TPU v7x, 32 devices: a whole 2x2x4 slice. The times are simulated.
32 devices in a mesh: pipe: 4 (over x, core), dp: 2 (over y), tensor: 4 (over z).
Axes of the slice: x: 2, y: 2, z: 4, core: 2. Of those that a mesh axis runs over, the one named last changes fastest.
Arguments:
- grad_top: bfloat16 [2, 128, 12288], P(None, None, ('dp', 'tensor')), may hold values from -1.1953125 to 1.1953125
- inputs: bfloat16 [4, 2, 128, 12288], P('pipe', None, None, ('dp', 'tensor')), may hold values from -6 to 6
- pre: bfloat16 [4, 2, 128, 6144], P('pipe', None, 'dp', 'tensor'), may hold values from -6 to 6
- weight_in: bfloat16 [4, 6144, 12288], P('pipe', 'tensor', 'dp'), may hold values from -0.0546875 to 0.0546875
- weight_out: bfloat16 [4, 6144, 12288], P('pipe', 'tensor', 'dp'), may hold values from -0.0546875 to 0.0546875
Outputs:
- weight_in_grad: bfloat16 [4, 6144, 12288], P('pipe', 'tensor', 'dp')
- weight_out_grad: bfloat16 [4, 6144, 12288], P('pipe', 'tensor', 'dp')
- section_grads: bfloat16 [4, 2, 128, 12288], P('pipe', None, None, ('dp', 'tensor'))
All inputs are finite; a program needn't handle non-finite values.
Results may differ from a plain program's by a relative error of at most 0.024.
Values may be sent and summed in bfloat16 or wider, within the bound.
A program may use at most 512 MiB of HBM per device.

v0:
```python
import math
import jax
import jax.numpy as jnp
from jax import lax
from jax.sharding import PartitionSpec as P


def shifted(block, axis, distance):
    devices = range(lax.axis_size(axis))
    route = [(i - distance, i) for i in devices if i - distance in devices]
    return lax.ppermute(block, axis, route)


def gelu_pair(values):
    root_coef = math.sqrt(2.0 / math.pi)
    inner = root_coef * (values + 0.044715 * values * values * values)
    tangent = jnp.tanh(inner)
    activ = 0.5 * values * (1.0 + tangent)
    slope = 0.5 * (1.0 + tangent) + 0.5 * values * (1.0 - tangent * tangent) * root_coef * (
        1.0 + 3.0 * 0.044715 * values * values
    )
    return (activ, slope)


def on_device(grad_top, inputs, pre, weight_in, weight_out):
    sections = lax.axis_size("pipe")
    section = lax.axis_index("pipe")
    micro = grad_top.shape[0]
    local_in = weight_in[0]
    local_out = weight_out[0]
    contract = (((0,), (0,)), ((), ()))
    accum_in = jnp.zeros(local_in.shape, jnp.float32)
    accum_out = jnp.zeros(local_out.shape, jnp.float32)
    grads_out = jnp.zeros(grad_top.shape, jnp.bfloat16)
    outgoing = grad_top[0]
    for timestep in range(micro + sections - 1):
        micro_index = timestep - (sections - 1 - section)
        valid = jnp.logical_and(micro_index >= 0, micro_index < micro)
        clipped = jnp.clip(micro_index, 0, micro - 1)
        top_grad = lax.dynamic_index_in_dim(grad_top, clipped, 0, False)
        if timestep == 0:
            current = top_grad
        else:
            received = shifted(outgoing, "pipe", -1)
            current = jnp.where(section == sections - 1, top_grad, received)
        layer_input = lax.dynamic_index_in_dim(inputs[0], clipped, 0, False)
        pre_local = lax.dynamic_index_in_dim(pre[0], clipped, 0, False)
        grad_cols, input_cols = (
            lax.all_gather(current, "tensor", axis=1, tiled=True),
            lax.all_gather(layer_input, "tensor", axis=1, tiled=True),
        )
        head_part = lax.dot_general(
            grad_cols, local_out, (((1,), (1,)), ((), ())), preferred_element_type=jnp.float32
        )
        head_grad = lax.psum(head_part.astype(jnp.bfloat16), "dp").astype(jnp.float32)
        pre_all = lax.all_gather(pre_local, "dp", axis=0, tiled=True)
        activ, slope = gelu_pair(pre_all.astype(jnp.float32))
        head_delta = (head_grad * slope).astype(jnp.bfloat16)
        activated = activ.astype(jnp.bfloat16)
        partial_value = jnp.dot(head_delta, local_in, preferred_element_type=jnp.float32)
        summed = lax.psum_scatter(
            partial_value.astype(jnp.bfloat16), "tensor", scatter_dimension=1, tiled=True
        ).astype(jnp.float32)
        new_grad = (current.astype(jnp.float32) + summed).astype(jnp.bfloat16)
        out_term = lax.dot_general(
            activated, grad_cols, contract, preferred_element_type=jnp.float32
        )
        in_term = lax.dot_general(
            head_delta, input_cols, contract, preferred_element_type=jnp.float32
        )
        accum_out = accum_out + jnp.where(valid, out_term, 0.0)
        accum_in = accum_in + jnp.where(valid, in_term, 0.0)
        previous = lax.dynamic_index_in_dim(grads_out, clipped, 0, False)
        grads_out = lax.dynamic_update_index_in_dim(
            grads_out, jnp.where(valid, new_grad, previous), clipped, 0
        )
        outgoing = new_grad
    return (
        accum_in.astype(jnp.bfloat16)[None],
        accum_out.astype(jnp.bfloat16)[None],
        grads_out[None],
    )


def solution(mesh):
    placed = (
        P(None, None, ("dp", "tensor")),
        P("pipe", None, None, ("dp", "tensor")),
        P("pipe", None, "dp", "tensor"),
        P("pipe", "tensor", "dp"),
        P("pipe", "tensor", "dp"),
    )
    return jax.shard_map(
        on_device,
        mesh=mesh,
        in_specs=placed,
        out_specs=(
            P("pipe", "tensor", "dp"),
            P("pipe", "tensor", "dp"),
            P("pipe", None, None, ("dp", "tensor")),
        ),
        check_vma=False,
    )
```

profile of v0, /device:TPU:0, one launch (start us, length us, event | category | flops | bytes accessed | tf_op | source)
XLA Modules:
  0.0 836.4 jit_solution(14600435980791823250)
XLA Ops:
  7.2 1.8 constant_dynamic-slice_fusion.13
  9.1 40.8 %all-gather.30.cloned.1.call-done = bf16[1,128,6144]{2,1,0:T(8,128)(2,1)} async-done(((bf16[1,128,1536]{2,1,0:T(8,128)(2,1)}), bf16[1,128,6144]{2,1,0:T(8,128)(2,1)}) %all-gather.30.cloned.1.call-update) | async-done | bytes 1572880 | tf_op jit(solution)/shard_map/all_gather | solution.py:49
  49.9 14.0 %fusion.37 = bf16[128,1536]{1,0:T(8,128)(2,1)} fusion(bf16[1,1536,6144]{2,1,0:T(8,128)(2,1)} %param.9, bf16[1,128,6144]{2,1,0:T(8,128)(2,1)} %all-gather.30.cloned.1.call-done), kind=kOutput, calls=%fused_computation.29 | convolution fusion | flops 2416115712 | bytes 20840448 | tf_op jit(solution)/shard_map/dot_general | solution.py:52
  64.0 0.8 constant_dynamic-slice_fusion.4
  64.8 9.4 %all-gather.1 = bf16[1,1,128,1536]{3,2,1,0:T(8,128)(2,1)S(1)} all-gather(bf16[1,1,64,1536]{3,2,1,0:T(8,128)(2,1)S(1)} %get-tuple-element.19), channel_id=3, replica_groups=mesh['pipe'=4,'dp'=2,'tensor'=4] {'dp'}, dimensions={2}, use_global_device_ids=true | all-gather | bytes 589824 | tf_op jit(solution)/shard_map/all_gather | solution.py:56
  74.2 15.2 %all-reduce.6.cloned.1.call-done = bf16[128,1536]{1,0:T(8,128)(2,1)} async-done(((bf16[128,1536]{1,0:T(8,128)(2,1)}), bf16[128,1536]{1,0:T(8,128)(2,1)}) %all-reduce.6.cloned.1.call-update) | async-done | bytes 393232 | tf_op jit(solution)/shard_map/psum | solution.py:55
  89.5 10.7 %fusion.22 = bf16[128,6144]{1,0:T(8,128)(2,1)} fusion(bf16[1,1536,6144]{2,1,0:T(8,128)(2,1)} %param.8, bf16[128,1536]{1,0:T(8,128)(2,1)} %all-reduce.6.cloned.1.call-done, bf16[1,1,128,1536]{3,2,1,0:T(8,128)(2,1)S(1)} %all-gather.1), kind=kOutput, calls=%fused_computation.24 | convolution fusion | flops 2420834304 | bytes 21233664 | tf_op jit(solution)/shard_map/dot_general | solution.py:60
  100.2 35.5 %reduce-scatter.6.cloned.1.call-done = bf16[128,1536]{1,0:T(8,128)(2,1)} async-done(((bf16[128,6144]{1,0:T(8,128)(2,1)}), bf16[128,1536]{1,0:T(8,128)(2,1)}) %reduce-scatter.6.cloned.1.call-update) | async-done | bytes 393232 | tf_op jit(solution)/shard_map/reduce_scatter | solution.py:61
  135.8 1.1 bitcast_dynamic-update-slice_fusion.3
  137.0 1.3 collective-permute-start
  138.3 2.3 collective-permute-done
  140.6 0.8 bitcast_select_fusion.6
  141.7 39.8 %all-gather.22.cloned.1.call-done = bf16[128,6144]{1,0:T(8,128)(2,1)} async-done(((bf16[128,1536]{1,0:T(8,128)(2,1)}), bf16[128,6144]{1,0:T(8,128)(2,1)}) %all-gather.22.cloned.1.call-update) | async-done | bytes 1572880 | tf_op jit(solution)/shard_map/all_gather | solution.py:49
  181.5 14.0 %fusion.40 = bf16[128,1536]{1,0:T(8,128)(2,1)} fusion(bf16[128,6144]{1,0:T(8,128)(2,1)} %all-gather.22.cloned.1.call-done, bf16[1,1536,6144]{2,1,0:T(8,128)(2,1)} %param.9), kind=kOutput, calls=%fused_computation.30 | convolution fusion | flops 2416115712 | bytes 20840448 | tf_op jit(solution)/shard_map/dot_general | solution.py:52
  195.6 8.2 all-gather.3
  203.8 16.6 %all-reduce.8.cloned.1.call-done = bf16[128,1536]{1,0:T(8,128)(2,1)} async-done(((bf16[128,1536]{1,0:T(8,128)(2,1)}), bf16[128,1536]{1,0:T(8,128)(2,1)}) %all-reduce.8.cloned.1.call-update) | async-done | bytes 393232 | tf_op jit(solution)/shard_map/psum | solution.py:55
  220.4 10.7 %fusion.25 = bf16[128,6144]{1,0:T(8,128)(2,1)} fusion(bf16[1,1536,6144]{2,1,0:T(8,128)(2,1)} %param.8, bf16[128,1536]{1,0:T(8,128)(2,1)} %all-reduce.8.cloned.1.call-done, bf16[1,1,128,1536]{3,2,1,0:T(8,128)(2,1)S(1)} %all-gather.3), kind=kOutput, calls=%fused_computation.25 | convolution fusion | flops 2420834304 | bytes 21233664 | tf_op jit(solution)/shard_map/dot_general | solution.py:60
  231.2 35.5 %reduce-scatter.8.cloned.1.call-done = bf16[128,1536]{1,0:T(8,128)(2,1)} async-done(((bf16[128,6144]{1,0:T(8,128)(2,1)}), bf16[128,1536]{1,0:T(8,128)(2,1)}) %reduce-scatter.8.cloned.1.call-update) | async-done | bytes 393232 | tf_op jit(solution)/shard_map/reduce_scatter | solution.py:61
  266.7 1.2 bitcast_dynamic-update-slice_fusion.2
  267.9 1.3 collective-permute-start.1
  269.2 2.3 collective-permute-done.1
  272.9 39.5 %all-gather.24.cloned.1.call-done = bf16[128,6144]{1,0:T(8,128)(2,1)} async-done(((bf16[128,1536]{1,0:T(8,128)(2,1)}), bf16[128,6144]{1,0:T(8,128)(2,1)}) %all-gather.24.cloned.1.call-update) | async-done | bytes 1572880 | tf_op jit(solution)/shard_map/all_gather | solution.py:49
  312.4 14.0 %fusion.43 = bf16[128,1536]{1,0:T(8,128)(2,1)} fusion(bf16[128,6144]{1,0:T(8,128)(2,1)} %all-gather.24.cloned.1.call-done, bf16[1,1536,6144]{2,1,0:T(8,128)(2,1)} %param.9), kind=kOutput, calls=%fused_computation.31 | convolution fusion | flops 2416115712 | bytes 20840448 | tf_op jit(solution)/shard_map/dot_general | solution.py:52
  326.5 8.3 all-gather.5
  334.7 16.6 %all-reduce.10.cloned.1.call-done = bf16[128,1536]{1,0:T(8,128)(2,1)} async-done(((bf16[128,1536]{1,0:T(8,128)(2,1)}), bf16[128,1536]{1,0:T(8,128)(2,1)}) %all-reduce.10.cloned.1.call-update) | async-done | bytes 393232 | tf_op jit(solution)/shard_map/psum | solution.py:55
  351.3 10.7 %fusion.28 = bf16[128,6144]{1,0:T(8,128)(2,1)} fusion(bf16[1,1536,6144]{2,1,0:T(8,128)(2,1)} %param.8, bf16[128,1536]{1,0:T(8,128)(2,1)} %all-reduce.10.cloned.1.call-done, bf16[1,1,128,1536]{3,2,1,0:T(8,128)(2,1)S(1)} %all-gather.5), kind=kOutput, calls=%fused_computation.26 | convolution fusion | flops 2420834304 | bytes 21233664 | tf_op jit(solution)/shard_map/dot_general | solution.py:60
  362.1 35.5 %reduce-scatter.10.cloned.1.call-done = bf16[128,1536]{1,0:T(8,128)(2,1)} async-done(((bf16[128,6144]{1,0:T(8,128)(2,1)}), bf16[128,1536]{1,0:T(8,128)(2,1)}) %reduce-scatter.10.cloned.1.call-update) | async-done | bytes 393232 | tf_op jit(solution)/shard_map/reduce_scatter | solution.py:61
  397.6 1.2 bitcast_dynamic-update-slice_fusion.1
  398.8 1.3 collective-permute-start.2
  400.1 2.3 collective-permute-done.2
  403.4 39.9 %all-gather.26.cloned.1.call-done = bf16[128,6144]{1,0:T(8,128)(2,1)} async-done(((bf16[128,1536]{1,0:T(8,128)(2,1)}), bf16[128,6144]{1,0:T(8,128)(2,1)}) %all-gather.26.cloned.1.call-update) | async-done | bytes 1572880 | tf_op jit(solution)/shard_map/all_gather | solution.py:49
  443.3 14.0 %fusion.46 = bf16[128,1536]{1,0:T(8,128)(2,1)} fusion(bf16[128,6144]{1,0:T(8,128)(2,1)} %all-gather.26.cloned.1.call-done, bf16[1,1536,6144]{2,1,0:T(8,128)(2,1)} %param.9), kind=kOutput, calls=%fused_computation.32 | convolution fusion | flops 2416115712 | bytes 20840448 | tf_op jit(solution)/shard_map/dot_general | solution.py:52
  457.3 7.8 all-gather.7
  465.2 16.9 %all-reduce.12.cloned.1.call-done = bf16[128,1536]{1,0:T(8,128)(2,1)} async-done(((bf16[128,1536]{1,0:T(8,128)(2,1)}), bf16[128,1536]{1,0:T(8,128)(2,1)}) %all-reduce.12.cloned.1.call-update) | async-done | bytes 393232 | tf_op jit(solution)/shard_map/psum | solution.py:55
  482.1 10.7 %fusion.31 = bf16[128,6144]{1,0:T(8,128)(2,1)} fusion(bf16[1,1536,6144]{2,1,0:T(8,128)(2,1)} %param.8, bf16[128,1536]{1,0:T(8,128)(2,1)} %all-reduce.12.cloned.1.call-done, bf16[1,1,128,1536]{3,2,1,0:T(8,128)(2,1)S(1)} %all-gather.7), kind=kOutput, calls=%fused_computation.27 | convolution fusion | flops 2420834304 | bytes 21233664 | tf_op jit(solution)/shard_map/dot_general | solution.py:60
  493.6 34.8 %reduce-scatter.12.cloned.1.call-done = bf16[128,1536]{1,0:T(8,128)(2,1)} async-done(((bf16[128,6144]{1,0:T(8,128)(2,1)}), bf16[128,1536]{1,0:T(8,128)(2,1)}) %reduce-scatter.12.cloned.1.call-update) | async-done | bytes 393232 | tf_op jit(solution)/shard_map/reduce_scatter | solution.py:61
  528.4 1.4 bitcast_dynamic-update-slice_fusion
  529.8 1.3 collective-permute-start.3
  531.1 2.3 collective-permute-done.3
  533.4 0.8 bitcast_select_fusion.3
  534.3 3.1 constant_dynamic-slice_fusion.3
  539.2 35.2 %all-gather.28.cloned.1.call-done = bf16[128,6144]{1,0:T(8,128)(2,1)} async-done(((bf16[128,1536]{1,0:T(8,128)(2,1)}), bf16[128,6144]{1,0:T(8,128)(2,1)}) %all-gather.28.cloned.1.call-update) | async-done | bytes 1572880 | tf_op jit(solution)/shard_map/all_gather | solution.py:49
  574.3 14.0 %fusion.49 = bf16[128,1536]{1,0:T(8,128)(2,1)} fusion(bf16[128,6144]{1,0:T(8,128)(2,1)} %all-gather.28.cloned.1.call-done, bf16[1,1536,6144]{2,1,0:T(8,128)(2,1)} %param.9), kind=kOutput, calls=%fused_computation.33 | convolution fusion | flops 2416115712 | bytes 20840448 | tf_op jit(solution)/shard_map/dot_general | solution.py:52
  589.2 6.7 all-gather.9
  595.9 14.9 %fusion.61 = f32[1536,6144]{1,0:T(8,128)} fusion(bf16[1,128,6144]{2,1,0:T(8,128)(2,1)S(1)} %copy-done.2, bf16[1,1,128,1536]{3,2,1,0:T(8,128)(2,1)S(1)} %all-gather.1), kind=kOutput, calls=%fused_computation.78 | convolution fusion | flops 2417885184 | bytes 39714816 | tf_op jit(solution)/shard_map/dot_general | solution.py:65
  610.8 0.8 all-gather.32.cloned.1.call-done
  611.7 16.8 %fusion.59 = f32[1536,6144]{1,0:T(8,128)} fusion(bf16[1,1,128,6144]{3,2,1,0:T(8,128)(2,1)} %all-gather.32.cloned.1.call-done, bf16[128,1536]{1,0:T(8,128)(2,1)} %all-reduce.6.cloned.1.call-done, bf16[1,1,128,1536]{3,2,1,0:T(8,128)(2,1)S(1)} %all-gather.1), kind=kOutput, calls=%fused_computation.76 | convolution fusion | flops 2420047872 | bytes 40108032 | tf_op jit(solution)/shard_map/dot_general | solution.py:68
  628.5 14.9 %fusion.121 = f32[1536,6144]{1,0:T(8,128)} fusion(bf16[128,6144]{1,0:T(8,128)(2,1)S(1)} %copy-done.3, bf16[1,1,128,1536]{3,2,1,0:T(8,128)(2,1)S(1)} %copy-done.7), kind=kOutput, calls=%fused_computation.142 | convolution fusion | flops 2417885184 | bytes 39714816 | tf_op jit(solution)/shard_map/dot_general | solution.py:65
  643.4 6.2 all-gather.34.cloned.1.call-done
  649.6 16.7 %fusion.57 = f32[1536,6144]{1,0:T(8,128)} fusion(bf16[1,1,128,6144]{3,2,1,0:T(8,128)(2,1)} %all-gather.34.cloned.1.call-done, bf16[128,1536]{1,0:T(8,128)(2,1)S(1)} %copy-done.20, bf16[1,1,128,1536]{3,2,1,0:T(8,128)(2,1)S(1)} %copy-done.7), kind=kOutput, calls=%fused_computation.74 | convolution fusion | flops 2420047872 | bytes 40108032 | tf_op jit(solution)/shard_map/dot_general | solution.py:68
  666.3 15.4 %fusion.123 = f32[1536,6144]{1,0:T(8,128)} fusion(bf16[128,6144]{1,0:T(8,128)(2,1)S(1)} %copy-done.4, bf16[1,1,128,1536]{3,2,1,0:T(8,128)(2,1)S(1)} %copy-done.9), kind=kOutput, calls=%fused_computation.143 | convolution fusion | flops 2417885184 | bytes 39714816 | tf_op jit(solution)/shard_map/dot_general | solution.py:65
  681.6 5.9 all-gather.36.cloned.1.call-done
  687.5 16.6 %fusion.55 = f32[1536,6144]{1,0:T(8,128)} fusion(bf16[1,1,128,6144]{3,2,1,0:T(8,128)(2,1)} %all-gather.36.cloned.1.call-done, bf16[128,1536]{1,0:T(8,128)(2,1)S(1)} %copy-done.21, bf16[1,1,128,1536]{3,2,1,0:T(8,128)(2,1)S(1)} %copy-done.9), kind=kOutput, calls=%fused_computation.72 | convolution fusion | flops 2420047872 | bytes 40108032 | tf_op jit(solution)/shard_map/dot_general | solution.py:68
  704.1 14.9 %fusion.125 = f32[1536,6144]{1,0:T(8,128)} fusion(bf16[128,6144]{1,0:T(8,128)(2,1)S(1)} %copy-done.5, bf16[1,1,128,1536]{3,2,1,0:T(8,128)(2,1)S(1)} %copy-done.11), kind=kOutput, calls=%fused_computation.144 | convolution fusion | flops 2417885184 | bytes 39714816 | tf_op jit(solution)/shard_map/dot_general | solution.py:65
  719.0 5.9 all-gather.38.cloned.1.call-done
  724.8 16.4 %fusion.53 = f32[1536,6144]{1,0:T(8,128)} fusion(bf16[1,1,128,6144]{3,2,1,0:T(8,128)(2,1)} %all-gather.38.cloned.1.call-done, bf16[128,1536]{1,0:T(8,128)(2,1)S(1)} %copy-done.22, bf16[1,1,128,1536]{3,2,1,0:T(8,128)(2,1)S(1)} %copy-done.11), kind=kOutput, calls=%fused_computation.70 | convolution fusion | flops 2420047872 | bytes 40108032 | tf_op jit(solution)/shard_map/dot_general | solution.py:68
  741.2 0.9 copy.17
  742.1 25.1 %fusion.1 = bf16[1,1536,6144]{2,1,0:T(8,128)(2,1)} fusion(bf16[128,6144]{1,0:T(8,128)(2,1)S(1)} %copy-done.1, f32[1536,6144]{1,0:T(8,128)} %fusion.125, f32[1536,6144]{1,0:T(8,128)} %fusion.123, f32[1536,6144]{1,0:T(8,128)} %fusion.121, f32[1536,6144]{1,0:T(8,128)} %fusion.61, pred[]{:T(512)S(6)} %and.20, pred[]{:T(512)S(6)} %and.19, pred[]{:T(512)S(6)} %and.18, ...), kind=kOutput, calls=%fused_computation.3 | convolution fusion | flops 2512257024 | bytes 171835392 | tf_op jit(solution)/shard_map/dot_general | solution.py:65
  767.3 10.8 %fusion.34 = bf16[128,6144]{1,0:T(8,128)(2,1)} fusion(bf16[1,1536,6144]{2,1,0:T(8,128)(2,1)} %param.8, bf16[128,1536]{1,0:T(8,128)(2,1)} %all-reduce.14.cloned.1.call-done, bf16[1,1,128,1536]{3,2,1,0:T(8,128)(2,1)S(1)} %copy-done.15), kind=kOutput, calls=%fused_computation.28 | convolution fusion | flops 2420834304 | bytes 21233664 | tf_op jit(solution)/shard_map/dot_general | solution.py:60
  778.1 12.7 %all-gather.40.cloned.1.call-done = bf16[1,1,128,6144]{3,2,1,0:T(8,128)(2,1)} async-done(((bf16[1,1,128,1536]{3,2,1,0:T(8,128)(2,1)}), bf16[1,1,128,6144]{3,2,1,0:T(8,128)(2,1)}) %all-gather.40.cloned.1.call-update) | async-done | bytes 1572880 | tf_op jit(solution)/shard_map/all_gather | solution.py:50
  790.9 25.9 %fusion = bf16[1,1536,6144]{2,1,0:T(8,128)(2,1)} fusion(f32[1536,6144]{1,0:T(8,128)} %fusion.53, f32[1536,6144]{1,0:T(8,128)} %fusion.55, f32[1536,6144]{1,0:T(8,128)} %fusion.57, f32[1536,6144]{1,0:T(8,128)} %fusion.59, pred[]{:T(512)S(6)} %and.20, pred[]{:T(512)S(6)} %and.19, pred[]{:T(512)S(6)} %and.18, pred[]{:T(512)S(6)} %and.17, pred[]{:T(512)S(6)} %and.16, ...), kind=kOutput, calls=%fused_computation.2 | convolution fusion | flops 2514419712 | bytes 172228608 | tf_op jit(solution)/shard_map/dot_general | solution.py:68
  816.8 10.6 %reduce-scatter.14.cloned.1.call-done = bf16[128,1536]{1,0:T(8,128)(2,1)} async-done(((bf16[128,6144]{1,0:T(8,128)(2,1)}), bf16[128,1536]{1,0:T(8,128)(2,1)}) %reduce-scatter.14.cloned.1.call-update) | async-done | bytes 393232 | tf_op jit(solution)/shard_map/reduce_scatter | solution.py:61
  827.3 1.1 fusion.130
  828.5 0.9 copy-done.18
  (94 shorter events, 7.0 us)
Async XLA Ops:
  7.2 56.8 %copy-start.16 = (bf16[1,2,64,1536]{3,2,1,0:T(8,128)(2,1)S(1)}, bf16[1,2,64,1536]{3,2,1,0:T(8,128)(2,1)}, u32[]{:S(2)}) copy-start(bf16[1,2,64,1536]{3,2,1,0:T(8,128)(2,1)} %param.7) | copy-start | bytes 1179652
  7.2 42.7 %all-gather.30.cloned.1.call-start = ((), (), s32[]{:S(2)}) async-start(), calls=%async_computation.19 | async-start | bytes 1966080 | tf_op jit(solution)/shard_map/all_gather | solution.py:49
  9.1 80.4 %all-reduce.6.cloned.1.call-start = ((), (), s32[]{:S(2)}) async-start(), calls=%async_computation.5 | async-start | bytes 786432 | tf_op jit(solution)/shard_map/psum | solution.py:55
  63.9 71.9 %copy-start = (bf16[2,128,1536]{2,1,0:T(8,128)(2,1)S(1)}, bf16[2,128,1536]{2,1,0:T(8,128)(2,1)}, u32[]{:S(2)}) copy-start(bf16[2,128,1536]{2,1,0:T(8,128)(2,1)} %param.5) | copy-start | bytes 2359300
  63.9 71.9 %reduce-scatter.6.cloned.1.call-start = ((), (), s32[]{:S(2)}) async-start(), calls=%async_computation.6 | async-start | bytes 1966080 | tf_op jit(solution)/shard_map/reduce_scatter | solution.py:61
  100.2 81.4 %all-gather.22.cloned.1.call-start = ((), (), s32[]{:S(2)}) async-start(), calls=%async_computation.7 | async-start | bytes 1966080 | tf_op jit(solution)/shard_map/all_gather | solution.py:49
  137.0 3.6 collective-permute-start
  141.4 79.0 %all-reduce.8.cloned.1.call-start = ((), (), s32[]{:S(2)}) async-start(), calls=%async_computation.8 | async-start | bytes 786432 | tf_op jit(solution)/shard_map/psum | solution.py:55
  195.5 71.2 %copy-start.12 = (bf16[128,1536]{1,0:T(8,128)(2,1)S(1)}, bf16[128,1536]{1,0:T(8,128)(2,1)}, u32[]{:S(2)}) copy-start(bf16[128,1536]{1,0:T(8,128)(2,1)} %bitcast_select_fusion.6) | copy-start | bytes 1179652
  195.5 71.2 %reduce-scatter.8.cloned.1.call-start = ((), (), s32[]{:S(2)}) async-start(), calls=%async_computation.9 | async-start | bytes 1966080 | tf_op jit(solution)/shard_map/reduce_scatter | solution.py:61
  203.8 122.6 %copy-start.6 = (bf16[1,1,128,1536]{3,2,1,0:T(8,128)(2,1)}, bf16[1,1,128,1536]{3,2,1,0:T(8,128)(2,1)S(1)}, u32[]{:S(2)}) copy-start(bf16[1,1,128,1536]{3,2,1,0:T(8,128)(2,1)S(1)} %all-gather.3) | copy-start | bytes 1179652
  231.1 81.3 %all-gather.24.cloned.1.call-start = ((), (), s32[]{:S(2)}) async-start(), calls=%async_computation.10 | async-start | bytes 1966080 | tf_op jit(solution)/shard_map/all_gather | solution.py:49
  267.9 3.6 collective-permute-start.1
  272.3 79.0 %all-reduce.10.cloned.1.call-start = ((), (), s32[]{:S(2)}) async-start(), calls=%async_computation.11 | async-start | bytes 786432 | tf_op jit(solution)/shard_map/psum | solution.py:55
  326.4 71.2 %copy-start.13 = (bf16[128,1536]{1,0:T(8,128)(2,1)S(1)}, bf16[128,1536]{1,0:T(8,128)(2,1)}, u32[]{:S(2)}) copy-start(bf16[128,1536]{1,0:T(8,128)(2,1)} %bitcast_select_fusion.5) | copy-start | bytes 1179652
  326.4 71.2 %reduce-scatter.10.cloned.1.call-start = ((), (), s32[]{:S(2)}) async-start(), calls=%async_computation.12 | async-start | bytes 1966080 | tf_op jit(solution)/shard_map/reduce_scatter | solution.py:61
  334.7 122.5 %copy-start.8 = (bf16[1,1,128,1536]{3,2,1,0:T(8,128)(2,1)}, bf16[1,1,128,1536]{3,2,1,0:T(8,128)(2,1)S(1)}, u32[]{:S(2)}) copy-start(bf16[1,1,128,1536]{3,2,1,0:T(8,128)(2,1)S(1)} %all-gather.5) | copy-start | bytes 1179652
  362.0 81.3 %all-gather.26.cloned.1.call-start = ((), (), s32[]{:S(2)}) async-start(), calls=%async_computation.13 | async-start | bytes 1966080 | tf_op jit(solution)/shard_map/all_gather | solution.py:49
  398.8 3.6 collective-permute-start.2
  403.2 78.9 %all-reduce.12.cloned.1.call-start = ((), (), s32[]{:S(2)}) async-start(), calls=%async_computation.14 | async-start | bytes 786432 | tf_op jit(solution)/shard_map/psum | solution.py:55
  457.3 71.1 %reduce-scatter.12.cloned.1.call-start = ((), (), s32[]{:S(2)}) async-start(), calls=%async_computation.15 | async-start | bytes 1966080 | tf_op jit(solution)/shard_map/reduce_scatter | solution.py:61
  465.2 16.9 %copy-start.10 = (bf16[1,1,128,1536]{3,2,1,0:T(8,128)(2,1)}, bf16[1,1,128,1536]{3,2,1,0:T(8,128)(2,1)S(1)}, u32[]{:S(2)}) copy-start(bf16[1,1,128,1536]{3,2,1,0:T(8,128)(2,1)S(1)} %all-gather.7) | copy-start | bytes 1179652
  492.7 103.2 %copy-start.2 = (bf16[1,128,6144]{2,1,0:T(8,128)(2,1)S(1)}, bf16[1,128,6144]{2,1,0:T(8,128)(2,1)}, u32[]{:S(2)}) copy-start(bf16[1,128,6144]{2,1,0:T(8,128)(2,1)} %all-gather.30.cloned.1.call-done) | copy-start | bytes 4718596
  492.8 81.5 %all-gather.28.cloned.1.call-start = ((), (), s32[]{:S(2)}) async-start(), calls=%async_computation.16 | async-start | bytes 1966080 | tf_op jit(solution)/shard_map/all_gather | solution.py:49
  529.8 3.6 collective-permute-start.3
  534.2 55.0 %copy-start.19 = (bf16[1,1,64,1536]{3,2,1,0:T(8,128)(2,1)S(1)}, bf16[1,1,64,1536]{3,2,1,0:T(8,128)(2,1)}, u32[]{:S(2)}) copy-start(bf16[1,1,64,1536]{3,2,1,0:T(8,128)(2,1)} %get-tuple-element.16) | copy-start | bytes 589828
  534.2 77.5 %all-gather.32.cloned.1.call-start = ((), (), s32[]{:S(2)}) async-start(), calls=%async_computation.20 | async-start | bytes 1966080 | tf_op jit(solution)/shard_map/all_gather | solution.py:50
  537.4 112.2 %all-gather.34.cloned.1.call-start = ((), (), s32[]{:S(2)}) async-start(), calls=%async_computation.21 | async-start | bytes 1966080 | tf_op jit(solution)/shard_map/all_gather | solution.py:50
  538.0 149.5 %all-gather.36.cloned.1.call-start = ((), (), s32[]{:S(2)}) async-start(), calls=%async_computation.22 | async-start | bytes 1966080 | tf_op jit(solution)/shard_map/all_gather | solution.py:50
  538.5 186.3 %all-gather.38.cloned.1.call-start = ((), (), s32[]{:S(2)}) async-start(), calls=%async_computation.23 | async-start | bytes 1966080 | tf_op jit(solution)/shard_map/all_gather | solution.py:50
  539.1 228.1 %all-reduce.14.cloned.1.call-start = ((), (), s32[]{:S(2)}) async-start(), calls=%async_computation.17 | async-start | bytes 786432 | tf_op jit(solution)/shard_map/psum | solution.py:55
  588.4 202.5 %all-gather.40.cloned.1.call-start = ((), (), s32[]{:S(2)}) async-start(), calls=%async_computation.24 | async-start | bytes 1966080 | tf_op jit(solution)/shard_map/all_gather | solution.py:50
  589.1 238.2 %reduce-scatter.14.cloned.1.call-start = ((), (), s32[]{:S(2)}) async-start(), calls=%async_computation.18 | async-start | bytes 1966080 | tf_op jit(solution)/shard_map/reduce_scatter | solution.py:61
  610.8 17.7 %copy-start.3 = (bf16[128,6144]{1,0:T(8,128)(2,1)S(1)}, bf16[128,6144]{1,0:T(8,128)(2,1)}, u32[]{:S(2)}) copy-start(bf16[128,6144]{1,0:T(8,128)(2,1)} %all-gather.22.cloned.1.call-done) | copy-start | bytes 4718596
  610.8 17.7 %copy-start.7 = (bf16[1,1,128,1536]{3,2,1,0:T(8,128)(2,1)S(1)}, bf16[1,1,128,1536]{3,2,1,0:T(8,128)(2,1)}, u32[]{:S(2)}) copy-start(bf16[1,1,128,1536]{3,2,1,0:T(8,128)(2,1)} %copy-done.6) | copy-start | bytes 1179652
  628.5 21.1 %copy-start.20 = (bf16[128,1536]{1,0:T(8,128)(2,1)S(1)}, bf16[128,1536]{1,0:T(8,128)(2,1)}, u32[]{:S(2)}) copy-start(bf16[128,1536]{1,0:T(8,128)(2,1)} %all-reduce.8.cloned.1.call-done) | copy-start | bytes 1179652
  643.4 22.9 %copy-start.4 = (bf16[128,6144]{1,0:T(8,128)(2,1)S(1)}, bf16[128,6144]{1,0:T(8,128)(2,1)}, u32[]{:S(2)}) copy-start(bf16[128,6144]{1,0:T(8,128)(2,1)} %all-gather.24.cloned.1.call-done) | copy-start | bytes 4718596
  643.4 22.9 %copy-start.9 = (bf16[1,1,128,1536]{3,2,1,0:T(8,128)(2,1)S(1)}, bf16[1,1,128,1536]{3,2,1,0:T(8,128)(2,1)}, u32[]{:S(2)}) copy-start(bf16[1,1,128,1536]{3,2,1,0:T(8,128)(2,1)} %copy-done.8) | copy-start | bytes 1179652
  666.3 21.2 %copy-start.21 = (bf16[128,1536]{1,0:T(8,128)(2,1)S(1)}, bf16[128,1536]{1,0:T(8,128)(2,1)}, u32[]{:S(2)}) copy-start(bf16[128,1536]{1,0:T(8,128)(2,1)} %all-reduce.10.cloned.1.call-done) | copy-start | bytes 1179652
  681.6 22.5 %copy-start.5 = (bf16[128,6144]{1,0:T(8,128)(2,1)S(1)}, bf16[128,6144]{1,0:T(8,128)(2,1)}, u32[]{:S(2)}) copy-start(bf16[128,6144]{1,0:T(8,128)(2,1)} %all-gather.26.cloned.1.call-done) | copy-start | bytes 4718596
  681.6 22.5 %copy-start.11 = (bf16[1,1,128,1536]{3,2,1,0:T(8,128)(2,1)S(1)}, bf16[1,1,128,1536]{3,2,1,0:T(8,128)(2,1)}, u32[]{:S(2)}) copy-start(bf16[1,1,128,1536]{3,2,1,0:T(8,128)(2,1)} %copy-done.10) | copy-start | bytes 1179652
  704.1 20.7 %copy-start.22 = (bf16[128,1536]{1,0:T(8,128)(2,1)S(1)}, bf16[128,1536]{1,0:T(8,128)(2,1)}, u32[]{:S(2)}) copy-start(bf16[128,1536]{1,0:T(8,128)(2,1)} %all-reduce.12.cloned.1.call-done) | copy-start | bytes 1179652
  719.0 23.2 %copy-start.1 = (bf16[128,6144]{1,0:T(8,128)(2,1)S(1)}, bf16[128,6144]{1,0:T(8,128)(2,1)}, u32[]{:S(2)}) copy-start(bf16[128,6144]{1,0:T(8,128)(2,1)} %all-gather.28.cloned.1.call-done) | copy-start | bytes 4718596
  719.0 23.2 %copy-start.15 = (bf16[1,1,128,1536]{3,2,1,0:T(8,128)(2,1)S(1)}, bf16[1,1,128,1536]{3,2,1,0:T(8,128)(2,1)}, u32[]{:S(2)}) copy-start(bf16[1,1,128,1536]{3,2,1,0:T(8,128)(2,1)} %all-gather.9) | copy-start | bytes 1179652
  767.2 23.6 %copy-start.23 = (bf16[128,1536]{1,0:T(8,128)(2,1)S(1)}, bf16[128,1536]{1,0:T(8,128)(2,1)}, u32[]{:S(2)}) copy-start(bf16[128,1536]{1,0:T(8,128)(2,1)} %all-reduce.14.cloned.1.call-done) | copy-start | bytes 1179652
  778.1 49.2 %copy-start.14 = (bf16[128,1536]{1,0:T(8,128)(2,1)S(1)}, bf16[128,1536]{1,0:T(8,128)(2,1)}, u32[]{:S(2)}) copy-start(bf16[128,1536]{1,0:T(8,128)(2,1)} %bitcast_select_fusion.3) | copy-start | bytes 1179652
  778.1 49.2 %copy-start.17 = (bf16[1,2,128,1536]{3,2,1,0:T(8,128)(2,1)S(1)}, bf16[1,2,128,1536]{3,2,1,0:T(8,128)(2,1)}, u32[]{:S(2)}) copy-start(bf16[1,2,128,1536]{3,2,1,0:T(8,128)(2,1)} %copy.17) | copy-start | bytes 2359300
  828.5 0.9 copy-start.18
Sparse Core Ops, SparseCore 0:
  10.1 39.7 all-gather.29
  64.0 25.3 all-reduce.5
  100.3 35.4 reduce-scatter.5
  141.5 39.9 all-gather.21
  195.6 24.7 all-reduce.7
  231.2 35.4 reduce-scatter.7
  272.4 39.9 all-gather.23
  326.5 24.7 all-reduce.9
  362.1 35.4 reduce-scatter.9
  403.3 39.9 all-gather.25
  457.4 24.6 all-reduce.11
  492.9 35.4 reduce-scatter.11
  534.3 39.9 all-gather.27
  575.7 35.8 all-gather.31
  613.6 35.8 all-gather.33
  651.6 35.8 all-gather.35
  688.9 35.8 all-gather.37
  727.0 24.6 all-reduce.13
  753.8 37.0 all-gather.39
  793.0 34.2 reduce-scatter.13
where the time goes:
time: 843 us; the launch traced here: 836 us
  waiting for transfers between devices  456 us (54%)
  matrix products  301 us (36%)
  blocking collectives  40.5 us (5%)
  between operations  14.8 us (2%)
  other arithmetic  9.16 us (1%)
  local copies, waits for them, and re-layouts  8.44 us (1%)
    all_gather x5, waiting for transfers between devices, on_device(): lax.all_gather(current, 'tensor', axis=1, tiled=True)  195 us
    reduce_scatter x5, waiting for transfers between devices, on_device(): lax.psum_scatter(partial_value.astype(jnp.bfloat16), 'tensor', scatter_di...  152 us
    dot_general x5, matrix products, on_device(): lax.dot_general(head_delta, input_cols, contract, preferred_element_type=...  92.4 us
    dot_general x5, matrix products, on_device(): lax.dot_general(activated, grad_cols, contract, preferred_element_type=jn...  85.1 us
    dot_general x5, matrix products, on_device(): lax.dot_general(grad_cols, local_out, (((1,), (1,)), ((), ())), preferred...  69.8 us
    psum x5, waiting for transfers between devices, on_device(): lax.psum(head_part.astype(jnp.bfloat16), 'dp').astype(jnp.float32)  65.3 us
    dot_general x5, matrix products, on_device(): jnp.dot(head_delta, local_in, preferred_element_type=jnp.float32)  53.6 us
    all_gather x5, blocking collectives, on_device(): pre_all = lax.all_gather(pre_local, 'dp', axis=0, tiled=True)  40.5 us
  transfers between devices with their start and end apart: 24, of which 23 were waited for; matrix products, arithmetic and copies ran while one was open for 25% of the time, Pallas kernels for 0%

commit v1 on v0

--- a/solution.py
+++ b/solution.py
@@ -52,7 +52,9 @@
         head_part = lax.dot_general(
             grad_cols, local_out, (((1,), (1,)), ((), ())), preferred_element_type=jnp.float32
         )
-        head_grad = lax.psum(head_part.astype(jnp.bfloat16), "dp").astype(jnp.float32)
+        head_grad = jnp.sum(lax.all_gather(head_part.astype(jnp.bfloat16), "dp"), 0).astype(
+            jnp.float32
+        )
         pre_all = lax.all_gather(pre_local, "dp", axis=0, tiled=True)
         activ, slope = gelu_pair(pre_all.astype(jnp.float32))
         head_delta = (head_grad * slope).astype(jnp.bfloat16)

time: 843 us -> 778 us (0.923)
  the two profiles are of different devices: /device:TPU:0 before, /device:TPU:1 now
where the time goes in v1:
time: 778 us; the launch traced here: 771 us
  waiting for transfers between devices  328 us (42%)
  matrix products  313 us (40%)
  blocking collectives  80.9 us (10%)
  between operations  14.7 us (2%)
  other arithmetic  13.2 us (2%)
  starting transfers between devices  12.6 us (2%)
  local copies, waits for them, and re-layouts  8.74 us (1%)
    reduce_scatter x5, waiting for transfers between devices, on_device(): lax.psum_scatter(partial_value.astype(jnp.bfloat16), 'tensor', scatter_di...  141 us
    all_gather x5, waiting for transfers between devices, on_device(): lax.all_gather(current, 'tensor', axis=1, tiled=True)  134 us
    dot_general x5, matrix products, on_device(): lax.dot_general(head_delta, input_cols, contract, preferred_element_type=...  100 us
    dot_general x5, matrix products, on_device(): lax.dot_general(activated, grad_cols, contract, preferred_element_type=jn...  91.6 us
    dot_general x5, matrix products, on_device(): lax.dot_general(grad_cols, local_out, (((1,), (1,)), ((), ())), preferred...  67.5 us
    dot_general x5, matrix products, on_device(): jnp.dot(head_delta, local_in, preferred_element_type=jnp.float32)  53.7 us
    all_gather x5, blocking collectives, on_device(): lax.all_gather(head_part.astype(jnp.bfloat16), 'dp')  49.8 us
    all_gather x5, blocking collectives, on_device(): pre_all = lax.all_gather(pre_local, 'dp', axis=0, tiled=True)  31.1 us
  transfers between devices with their start and end apart: 19, of which 18 were waited for; matrix products, arithmetic and copies ran while one was open for 29% of the time, Pallas kernels for 0%

profile of v1, /device:TPU:1, one launch (start us, length us, event | category | flops | bytes accessed | tf_op | source)
XLA Modules:
  0.0 771.1 jit_solution(14199324521474197440)
XLA Ops:
  7.2 1.8 constant_dynamic-slice_fusion.13
  9.1 2.1 constant_dynamic-slice_fusion.4
  11.2 7.2 all-gather.2
  18.4 29.9 %all-gather.35.cloned.1.call-done = bf16[1,128,6144]{2,1,0:T(8,128)(2,1)} async-done(((bf16[1,128,1536]{2,1,0:T(8,128)(2,1)}), bf16[1,128,6144]{2,1,0:T(8,128)(2,1)}) %all-gather.35.cloned.1.call-update) | async-done | bytes 1572880 | tf_op jit(solution)/shard_map/all_gather | solution.py:49
  48.4 13.2 %fusion.37 = bf16[128,1536]{1,0:T(8,128)(2,1)S(1)} fusion(bf16[1,1536,6144]{2,1,0:T(8,128)(2,1)} %param.9, bf16[1,128,6144]{2,1,0:T(8,128)(2,1)} %all-gather.35.cloned.1.call-done), kind=kOutput, calls=%fused_computation.29 | convolution fusion | flops 2416115712 | bytes 20840448 | tf_op jit(solution)/shard_map/dot_general | solution.py:52
  61.6 9.9 %all-gather.1 = bf16[256,1536]{1,0:T(8,128)(2,1)S(1)} all-gather(bf16[128,1536]{1,0:T(8,128)(2,1)S(1)} %fusion.37), channel_id=3, replica_groups=mesh['pipe'=4,'dp'=2,'tensor'=4] {'dp'}, dimensions={0}, use_global_device_ids=true | all-gather | bytes 1179648 | tf_op jit(solution)/shard_map/all_gather | solution.py:55
  71.7 10.7 %fusion.22 = bf16[128,6144]{1,0:T(8,128)(2,1)} fusion(bf16[1,1536,6144]{2,1,0:T(8,128)(2,1)} %param.8, bf16[128,1536]{1,0:T(8,128)(2,1)S(1)} %reduce_sum.60, bf16[1,1,128,1536]{3,2,1,0:T(8,128)(2,1)S(1)} %all-gather.2), kind=kOutput, calls=%fused_computation.24 | convolution fusion | flops 2420834304 | bytes 21233664 | tf_op jit(solution)/shard_map/dot_general | solution.py:62
  82.4 36.7 %reduce-scatter.6.cloned.1.call-done = bf16[128,1536]{1,0:T(8,128)(2,1)} async-done(((bf16[128,6144]{1,0:T(8,128)(2,1)}), bf16[128,1536]{1,0:T(8,128)(2,1)}) %reduce-scatter.6.cloned.1.call-update) | async-done | bytes 393232 | tf_op jit(solution)/shard_map/reduce_scatter | solution.py:63
  119.2 1.1 bitcast_dynamic-update-slice_fusion.3
  120.4 3.0 collective-permute-start
  123.4 6.8 collective-permute-done
  131.0 5.4 all-gather.5
  136.4 28.3 %all-gather.27.cloned.1.call-done = bf16[128,6144]{1,0:T(8,128)(2,1)} async-done(((bf16[128,1536]{1,0:T(8,128)(2,1)}), bf16[128,6144]{1,0:T(8,128)(2,1)}) %all-gather.27.cloned.1.call-update) | async-done | bytes 1572880 | tf_op jit(solution)/shard_map/all_gather | solution.py:49
  164.7 14.0 %fusion.40 = bf16[128,1536]{1,0:T(8,128)(2,1)} fusion(bf16[128,6144]{1,0:T(8,128)(2,1)} %all-gather.27.cloned.1.call-done, bf16[1,1536,6144]{2,1,0:T(8,128)(2,1)} %param.9), kind=kOutput, calls=%fused_computation.30 | convolution fusion | flops 2416115712 | bytes 20840448 | tf_op jit(solution)/shard_map/dot_general | solution.py:52
  178.7 10.1 %all-gather.4 = bf16[256,1536]{1,0:T(8,128)(2,1)S(1)} all-gather(bf16[128,1536]{1,0:T(8,128)(2,1)} %fusion.40), channel_id=6, replica_groups=mesh['pipe'=4,'dp'=2,'tensor'=4] {'dp'}, dimensions={0}, use_global_device_ids=true | all-gather | bytes 1179648 | tf_op jit(solution)/shard_map/all_gather | solution.py:55
  188.8 1.0 reduce_sum.61
  189.8 10.7 %fusion.25 = bf16[128,6144]{1,0:T(8,128)(2,1)} fusion(bf16[1,1536,6144]{2,1,0:T(8,128)(2,1)} %param.8, bf16[128,1536]{1,0:T(8,128)(2,1)} %reduce_sum.61, bf16[1,1,128,1536]{3,2,1,0:T(8,128)(2,1)S(1)} %all-gather.5), kind=kOutput, calls=%fused_computation.25 | convolution fusion | flops 2420834304 | bytes 21233664 | tf_op jit(solution)/shard_map/dot_general | solution.py:62
  200.6 36.7 %reduce-scatter.8.cloned.1.call-done = bf16[128,1536]{1,0:T(8,128)(2,1)} async-done(((bf16[128,6144]{1,0:T(8,128)(2,1)}), bf16[128,1536]{1,0:T(8,128)(2,1)}) %reduce-scatter.8.cloned.1.call-update) | async-done | bytes 393232 | tf_op jit(solution)/shard_map/reduce_scatter | solution.py:63
  237.3 1.2 bitcast_dynamic-update-slice_fusion.2
  238.5 3.0 collective-permute-start.1
  241.4 6.8 collective-permute-done.1
  249.1 5.4 all-gather.8
  254.6 28.2 %all-gather.29.cloned.1.call-done = bf16[128,6144]{1,0:T(8,128)(2,1)} async-done(((bf16[128,1536]{1,0:T(8,128)(2,1)}), bf16[128,6144]{1,0:T(8,128)(2,1)}) %all-gather.29.cloned.1.call-update) | async-done | bytes 1572880 | tf_op jit(solution)/shard_map/all_gather | solution.py:49
  282.8 14.0 %fusion.43 = bf16[128,1536]{1,0:T(8,128)(2,1)} fusion(bf16[128,6144]{1,0:T(8,128)(2,1)} %all-gather.29.cloned.1.call-done, bf16[1,1536,6144]{2,1,0:T(8,128)(2,1)} %param.9), kind=kOutput, calls=%fused_computation.31 | convolution fusion | flops 2416115712 | bytes 20840448 | tf_op jit(solution)/shard_map/dot_general | solution.py:52
  296.8 10.1 %all-gather.7 = bf16[256,1536]{1,0:T(8,128)(2,1)S(1)} all-gather(bf16[128,1536]{1,0:T(8,128)(2,1)} %fusion.43), channel_id=9, replica_groups=mesh['pipe'=4,'dp'=2,'tensor'=4] {'dp'}, dimensions={0}, use_global_device_ids=true | all-gather | bytes 1179648 | tf_op jit(solution)/shard_map/all_gather | solution.py:55
  306.9 1.0 reduce_sum.62
  307.9 10.7 %fusion.28 = bf16[128,6144]{1,0:T(8,128)(2,1)} fusion(bf16[1,1536,6144]{2,1,0:T(8,128)(2,1)} %param.8, bf16[128,1536]{1,0:T(8,128)(2,1)} %reduce_sum.62, bf16[1,1,128,1536]{3,2,1,0:T(8,128)(2,1)S(1)} %all-gather.8), kind=kOutput, calls=%fused_computation.26 | convolution fusion | flops 2420834304 | bytes 21233664 | tf_op jit(solution)/shard_map/dot_general | solution.py:62
  318.7 36.7 %reduce-scatter.10.cloned.1.call-done = bf16[128,1536]{1,0:T(8,128)(2,1)} async-done(((bf16[128,6144]{1,0:T(8,128)(2,1)}), bf16[128,1536]{1,0:T(8,128)(2,1)}) %reduce-scatter.10.cloned.1.call-update) | async-done | bytes 393232 | tf_op jit(solution)/shard_map/reduce_scatter | solution.py:63
  355.4 1.2 bitcast_dynamic-update-slice_fusion.1
  356.6 3.0 collective-permute-start.2
  359.6 6.5 collective-permute-done.2
  367.0 5.8 all-gather.11
  372.7 27.9 %all-gather.31.cloned.1.call-done = bf16[128,6144]{1,0:T(8,128)(2,1)} async-done(((bf16[128,1536]{1,0:T(8,128)(2,1)}), bf16[128,6144]{1,0:T(8,128)(2,1)}) %all-gather.31.cloned.1.call-update) | async-done | bytes 1572880 | tf_op jit(solution)/shard_map/all_gather | solution.py:49
  400.6 13.2 %fusion.46 = bf16[128,1536]{1,0:T(8,128)(2,1)S(1)} fusion(bf16[128,6144]{1,0:T(8,128)(2,1)} %all-gather.31.cloned.1.call-done, bf16[1,1536,6144]{2,1,0:T(8,128)(2,1)} %param.9), kind=kOutput, calls=%fused_computation.32 | convolution fusion | flops 2416115712 | bytes 20840448 | tf_op jit(solution)/shard_map/dot_general | solution.py:52
  413.8 9.8 %all-gather.10 = bf16[256,1536]{1,0:T(8,128)(2,1)S(1)} all-gather(bf16[128,1536]{1,0:T(8,128)(2,1)S(1)} %fusion.46), channel_id=12, replica_groups=mesh['pipe'=4,'dp'=2,'tensor'=4] {'dp'}, dimensions={0}, use_global_device_ids=true | all-gather | bytes 1179648 | tf_op jit(solution)/shard_map/all_gather | solution.py:55
  423.6 1.0 reduce_sum.63
  424.6 10.9 %fusion.31 = bf16[128,6144]{1,0:T(8,128)(2,1)} fusion(bf16[1,1536,6144]{2,1,0:T(8,128)(2,1)} %param.8, bf16[128,1536]{1,0:T(8,128)(2,1)} %reduce_sum.63, bf16[1,1,128,1536]{3,2,1,0:T(8,128)(2,1)} %all-gather.11), kind=kOutput, calls=%fused_computation.27 | convolution fusion | flops 2420834304 | bytes 21233664 | tf_op jit(solution)/shard_map/dot_general | solution.py:62
  435.6 3.0 constant_dynamic-slice_fusion.3
  441.3 31.0 %reduce-scatter.12.cloned.1.call-done = bf16[128,1536]{1,0:T(8,128)(2,1)} async-done(((bf16[128,6144]{1,0:T(8,128)(2,1)}), bf16[128,1536]{1,0:T(8,128)(2,1)}) %reduce-scatter.12.cloned.1.call-update) | async-done | bytes 393232 | tf_op jit(solution)/shard_map/reduce_scatter | solution.py:63
  472.3 1.4 bitcast_dynamic-update-slice_fusion
  473.7 3.0 collective-permute-start.3
  476.7 6.5 collective-permute-done.3
  484.7 7.3 all-gather.14
  492.0 14.8 %fusion.61 = f32[1536,6144]{1,0:T(8,128)} fusion(bf16[1,128,6144]{2,1,0:T(8,128)(2,1)S(1)} %copy-done.2, bf16[1,1,128,1536]{3,2,1,0:T(8,128)(2,1)S(1)} %all-gather.2), kind=kOutput, calls=%fused_computation.78 | convolution fusion | flops 2417885184 | bytes 39714816 | tf_op jit(solution)/shard_map/dot_general | solution.py:67
  506.7 2.6 all-gather.37.cloned.1.call-done
  509.3 16.8 %fusion.59 = f32[1536,6144]{1,0:T(8,128)} fusion(bf16[1,1,128,6144]{3,2,1,0:T(8,128)(2,1)} %all-gather.37.cloned.1.call-done, bf16[128,1536]{1,0:T(8,128)(2,1)} %copy-done.15, bf16[1,1,128,1536]{3,2,1,0:T(8,128)(2,1)S(1)} %all-gather.2), kind=kOutput, calls=%fused_computation.76 | convolution fusion | flops 2420047872 | bytes 40108032 | tf_op jit(solution)/shard_map/dot_general | solution.py:70
  526.1 15.0 %fusion.121 = f32[1536,6144]{1,0:T(8,128)} fusion(bf16[128,6144]{1,0:T(8,128)(2,1)S(1)} %copy-done.3, bf16[1,1,128,1536]{3,2,1,0:T(8,128)(2,1)S(1)} %copy-done.7), kind=kOutput, calls=%fused_computation.142 | convolution fusion | flops 2417885184 | bytes 39714816 | tf_op jit(solution)/shard_map/dot_general | solution.py:67
  541.1 5.5 all-gather.39.cloned.1.call-done
  546.6 16.8 %fusion.57 = f32[1536,6144]{1,0:T(8,128)} fusion(bf16[1,1,128,6144]{3,2,1,0:T(8,128)(2,1)} %all-gather.39.cloned.1.call-done, bf16[128,1536]{1,0:T(8,128)(2,1)S(1)} %copy-done.16, bf16[1,1,128,1536]{3,2,1,0:T(8,128)(2,1)S(1)} %copy-done.7), kind=kOutput, calls=%fused_computation.74 | convolution fusion | flops 2420047872 | bytes 40108032 | tf_op jit(solution)/shard_map/dot_general | solution.py:70
  563.4 15.2 %fusion.123 = f32[1536,6144]{1,0:T(8,128)} fusion(bf16[128,6144]{1,0:T(8,128)(2,1)S(1)} %copy-done.4, bf16[1,1,128,1536]{3,2,1,0:T(8,128)(2,1)S(1)} %copy-done.9), kind=kOutput, calls=%fused_computation.143 | convolution fusion | flops 2417885184 | bytes 39714816 | tf_op jit(solution)/shard_map/dot_general | solution.py:67
  578.6 6.1 all-gather.41.cloned.1.call-done
  584.7 16.7 %fusion.55 = f32[1536,6144]{1,0:T(8,128)} fusion(bf16[1,1,128,6144]{3,2,1,0:T(8,128)(2,1)} %all-gather.41.cloned.1.call-done, bf16[128,1536]{1,0:T(8,128)(2,1)S(1)} %copy-done.17, bf16[1,1,128,1536]{3,2,1,0:T(8,128)(2,1)S(1)} %copy-done.9), kind=kOutput, calls=%fused_computation.72 | convolution fusion | flops 2420047872 | bytes 40108032 | tf_op jit(solution)/shard_map/dot_general | solution.py:70
  601.4 14.9 %fusion.125 = f32[1536,6144]{1,0:T(8,128)} fusion(bf16[128,6144]{1,0:T(8,128)(2,1)S(1)} %copy-done.5, bf16[1,1,128,1536]{3,2,1,0:T(8,128)(2,1)S(1)} %copy-done.10), kind=kOutput, calls=%fused_computation.144 | convolution fusion | flops 2417885184 | bytes 39714816 | tf_op jit(solution)/shard_map/dot_general | solution.py:67
  616.3 5.8 all-gather.43.cloned.1.call-done
  622.1 16.9 %fusion.53 = f32[1536,6144]{1,0:T(8,128)} fusion(bf16[1,1,128,6144]{3,2,1,0:T(8,128)(2,1)} %all-gather.43.cloned.1.call-done, bf16[128,1536]{1,0:T(8,128)(2,1)S(1)} %copy-done.18, bf16[1,1,128,1536]{3,2,1,0:T(8,128)(2,1)S(1)} %copy-done.10), kind=kOutput, calls=%fused_computation.70 | convolution fusion | flops 2420047872 | bytes 40108032 | tf_op jit(solution)/shard_map/dot_general | solution.py:70
  639.0 0.9 copy.12
  639.9 19.7 %all-gather.33.cloned.1.call-done = bf16[128,6144]{1,0:T(8,128)(2,1)} async-done(((bf16[128,1536]{1,0:T(8,128)(2,1)}), bf16[128,6144]{1,0:T(8,128)(2,1)}) %all-gather.33.cloned.1.call-update) | async-done | bytes 1572880 | tf_op jit(solution)/shard_map/all_gather | solution.py:49
  659.5 13.2 %fusion.49 = bf16[128,1536]{1,0:T(8,128)(2,1)S(1)} fusion(bf16[128,6144]{1,0:T(8,128)(2,1)} %all-gather.33.cloned.1.call-done, bf16[1,1536,6144]{2,1,0:T(8,128)(2,1)} %param.9), kind=kOutput, calls=%fused_computation.33 | convolution fusion | flops 2416115712 | bytes 20840448 | tf_op jit(solution)/shard_map/dot_general | solution.py:52
  672.7 9.9 %all-gather.13 = bf16[256,1536]{1,0:T(8,128)(2,1)S(1)} all-gather(bf16[128,1536]{1,0:T(8,128)(2,1)S(1)} %fusion.49), channel_id=15, replica_groups=mesh['pipe'=4,'dp'=2,'tensor'=4] {'dp'}, dimensions={0}, use_global_device_ids=true | all-gather | bytes 1179648 | tf_op jit(solution)/shard_map/all_gather | solution.py:55
  682.8 10.7 %fusion.34 = bf16[128,6144]{1,0:T(8,128)(2,1)} fusion(bf16[1,1536,6144]{2,1,0:T(8,128)(2,1)} %param.8, bf16[128,1536]{1,0:T(8,128)(2,1)S(1)} %reduce_sum.64, bf16[1,1,128,1536]{3,2,1,0:T(8,128)(2,1)S(1)} %copy-done.14), kind=kOutput, calls=%fused_computation.28 | convolution fusion | flops 2420834304 | bytes 21233664 | tf_op jit(solution)/shard_map/dot_general | solution.py:62
  693.5 3.9 all-gather.45.cloned.1.call-done
  697.5 33.0 %fusion = bf16[1,1536,6144]{2,1,0:T(8,128)(2,1)} fusion(f32[1536,6144]{1,0:T(8,128)} %fusion.53, f32[1536,6144]{1,0:T(8,128)} %fusion.55, f32[1536,6144]{1,0:T(8,128)} %fusion.57, f32[1536,6144]{1,0:T(8,128)} %fusion.59, pred[]{:T(512)S(6)} %and.20, pred[]{:T(512)S(6)} %and.19, pred[]{:T(512)S(6)} %and.18, pred[]{:T(512)S(6)} %and.17, pred[]{:T(512)S(6)} %and.16, ...), kind=kOutput, calls=%fused_computation.2 | convolution fusion | flops 2514419712 | bytes 172228608 | tf_op jit(solution)/shard_map/dot_general | solution.py:70
  730.4 31.8 %fusion.1 = bf16[1,1536,6144]{2,1,0:T(8,128)(2,1)} fusion(bf16[128,6144]{1,0:T(8,128)(2,1)S(1)} %copy-done.1, f32[1536,6144]{1,0:T(8,128)} %fusion.125, f32[1536,6144]{1,0:T(8,128)} %fusion.123, f32[1536,6144]{1,0:T(8,128)} %fusion.121, f32[1536,6144]{1,0:T(8,128)} %fusion.61, pred[]{:T(512)S(6)} %and.20, pred[]{:T(512)S(6)} %and.19, pred[]{:T(512)S(6)} %and.18, ...), kind=kOutput, calls=%fused_computation.3 | convolution fusion | flops 2512257024 | bytes 171835392 | tf_op jit(solution)/shard_map/dot_general | solution.py:67
  762.3 1.9 fusion.130
  (83 shorter events, 7.5 us)
Async XLA Ops:
  7.2 41.2 %all-gather.35.cloned.1.call-start = ((), (), s32[]{:S(2)}) async-start(), calls=%async_computation.14 | async-start | bytes 1966080 | tf_op jit(solution)/shard_map/all_gather | solution.py:49
  9.0 110.1 %reduce-scatter.6.cloned.1.call-start = ((), (), s32[]{:S(2)}) async-start(), calls=%async_computation.5 | async-start | bytes 1966080 | tf_op jit(solution)/shard_map/reduce_scatter | solution.py:63
  61.6 57.6 %copy-start = (bf16[2,128,1536]{2,1,0:T(8,128)(2,1)S(1)}, bf16[2,128,1536]{2,1,0:T(8,128)(2,1)}, u32[]{:S(2)}) copy-start(bf16[2,128,1536]{2,1,0:T(8,128)(2,1)} %param.5) | copy-start | bytes 2359300
  71.6 59.4 %copy-start.15 = (bf16[128,1536]{1,0:T(8,128)(2,1)}, bf16[128,1536]{1,0:T(8,128)(2,1)S(1)}, u32[]{:S(2)}) copy-start(bf16[128,1536]{1,0:T(8,128)(2,1)S(1)} %reduce_sum.60) | copy-start | bytes 1179652
  82.4 82.3 %all-gather.27.cloned.1.call-start = ((), (), s32[]{:S(2)}) async-start(), calls=%async_computation.6 | async-start | bytes 1966080 | tf_op jit(solution)/shard_map/all_gather | solution.py:49
  120.4 9.8 %collective-permute-start = (bf16[128,1536]{1,0:T(8,128)(2,1)S(1)}, bf16[128,1536]{1,0:T(8,128)(2,1)S(1)}, u32[]{:S(2)}, u32[]{:S(2)}) collective-permute-start(bf16[128,1536]{1,0:T(8,128)(2,1)S(1)} %get-tuple-element.10), channel_id=1, source_target_pairs={{8,0},{16,8},{24,16},{9,1},{17,9},{25,17},{10,2},{18,10},{26,18},{... | collective-permute-start | bytes 1179656 | tf_op jit(solution)/shard_map/ppermute | solution.py:11
  131.0 106.3 %reduce-scatter.8.cloned.1.call-start = ((), (), s32[]{:S(2)}) async-start(), calls=%async_computation.7 | async-start | bytes 1966080 | tf_op jit(solution)/shard_map/reduce_scatter | solution.py:63
  136.4 64.0 %copy-start.6 = (bf16[1,1,128,1536]{3,2,1,0:T(8,128)(2,1)}, bf16[1,1,128,1536]{3,2,1,0:T(8,128)(2,1)S(1)}, u32[]{:S(2)}) copy-start(bf16[1,1,128,1536]{3,2,1,0:T(8,128)(2,1)S(1)} %all-gather.5) | copy-start | bytes 1179652
  178.6 58.6 %copy-start.11 = (bf16[128,1536]{1,0:T(8,128)(2,1)S(1)}, bf16[128,1536]{1,0:T(8,128)(2,1)}, u32[]{:S(2)}) copy-start(bf16[128,1536]{1,0:T(8,128)(2,1)} %bitcast_select_fusion.6) | copy-start | bytes 1179652
  189.7 59.4 %copy-start.20 = (bf16[1,1,64,1536]{3,2,1,0:T(8,128)(2,1)S(1)}, bf16[1,1,64,1536]{3,2,1,0:T(8,128)(2,1)}, u32[]{:S(2)}) copy-start(bf16[1,1,64,1536]{3,2,1,0:T(8,128)(2,1)} %get-tuple-element.17) | copy-start | bytes 589828
  200.5 82.3 %all-gather.29.cloned.1.call-start = ((), (), s32[]{:S(2)}) async-start(), calls=%async_computation.8 | async-start | bytes 1966080 | tf_op jit(solution)/shard_map/all_gather | solution.py:49
  238.5 9.8 %collective-permute-start.1 = (bf16[128,1536]{1,0:T(8,128)(2,1)S(1)}, bf16[128,1536]{1,0:T(8,128)(2,1)S(1)}, u32[]{:S(2)}, u32[]{:S(2)}) collective-permute-start(bf16[128,1536]{1,0:T(8,128)(2,1)S(1)} %get-tuple-element.8), channel_id=1, source_target_pairs={{8,0},{16,8},{24,16},{9,1},{17,9},{25,17},{10,2},{18,10},{26,18},{... | collective-permute-start | bytes 1179656 | tf_op jit(solution)/shard_map/ppermute | solution.py:11
  249.1 106.3 %reduce-scatter.10.cloned.1.call-start = ((), (), s32[]{:S(2)}) async-start(), calls=%async_computation.9 | async-start | bytes 1966080 | tf_op jit(solution)/shard_map/reduce_scatter | solution.py:63
  254.6 64.0 %copy-start.8 = (bf16[1,1,128,1536]{3,2,1,0:T(8,128)(2,1)}, bf16[1,1,128,1536]{3,2,1,0:T(8,128)(2,1)S(1)}, u32[]{:S(2)}) copy-start(bf16[1,1,128,1536]{3,2,1,0:T(8,128)(2,1)S(1)} %all-gather.8) | copy-start | bytes 1179652
  296.8 58.6 %copy-start.12 = (bf16[128,1536]{1,0:T(8,128)(2,1)S(1)}, bf16[128,1536]{1,0:T(8,128)(2,1)}, u32[]{:S(2)}) copy-start(bf16[128,1536]{1,0:T(8,128)(2,1)} %bitcast_select_fusion.5) | copy-start | bytes 1179652
  307.9 59.1 %copy-start.19 = (bf16[1,1,64,1536]{3,2,1,0:T(8,128)(2,1)S(1)}, bf16[1,1,64,1536]{3,2,1,0:T(8,128)(2,1)}, u32[]{:S(2)}) copy-start(bf16[1,1,64,1536]{3,2,1,0:T(8,128)(2,1)} %get-tuple-element.20) | copy-start | bytes 589828
  318.6 82.0 %all-gather.31.cloned.1.call-start = ((), (), s32[]{:S(2)}) async-start(), calls=%async_computation.10 | async-start | bytes 1966080 | tf_op jit(solution)/shard_map/all_gather | solution.py:49
  356.6 9.5 %collective-permute-start.2 = (bf16[128,1536]{1,0:T(8,128)(2,1)S(1)}, bf16[128,1536]{1,0:T(8,128)(2,1)S(1)}, u32[]{:S(2)}, u32[]{:S(2)}) collective-permute-start(bf16[128,1536]{1,0:T(8,128)(2,1)S(1)} %get-tuple-element.6), channel_id=1, source_target_pairs={{8,0},{16,8},{24,16},{9,1},{17,9},{25,17},{10,2},{18,10},{26,18},{... | collective-permute-start | bytes 1179656 | tf_op jit(solution)/shard_map/ppermute | solution.py:11
  366.9 105.4 %reduce-scatter.12.cloned.1.call-start = ((), (), s32[]{:S(2)}) async-start(), calls=%async_computation.11 | async-start | bytes 1966080 | tf_op jit(solution)/shard_map/reduce_scatter | solution.py:63
  424.6 67.4 %copy-start.2 = (bf16[1,128,6144]{2,1,0:T(8,128)(2,1)S(1)}, bf16[1,128,6144]{2,1,0:T(8,128)(2,1)}, u32[]{:S(2)}) copy-start(bf16[1,128,6144]{2,1,0:T(8,128)(2,1)} %all-gather.35.cloned.1.call-done) | copy-start | bytes 4718596
  435.5 73.8 %all-gather.37.cloned.1.call-start = ((), (), s32[]{:S(2)}) async-start(), calls=%async_computation.15 | async-start | bytes 1966080 | tf_op jit(solution)/shard_map/all_gather | solution.py:50
  438.6 108.1 %all-gather.39.cloned.1.call-start = ((), (), s32[]{:S(2)}) async-start(), calls=%async_computation.16 | async-start | bytes 1966080 | tf_op jit(solution)/shard_map/all_gather | solution.py:50
  439.1 145.6 %all-gather.41.cloned.1.call-start = ((), (), s32[]{:S(2)}) async-start(), calls=%async_computation.17 | async-start | bytes 1966080 | tf_op jit(solution)/shard_map/all_gather | solution.py:50
  439.9 182.2 %all-gather.43.cloned.1.call-start = ((), (), s32[]{:S(2)}) async-start(), calls=%async_computation.18 | async-start | bytes 1966080 | tf_op jit(solution)/shard_map/all_gather | solution.py:50
  440.5 219.1 %all-gather.33.cloned.1.call-start = ((), (), s32[]{:S(2)}) async-start(), calls=%async_computation.12 | async-start | bytes 1966080 | tf_op jit(solution)/shard_map/all_gather | solution.py:49
  473.7 9.5 %collective-permute-start.3 = (bf16[128,1536]{1,0:T(8,128)(2,1)S(1)}, bf16[128,1536]{1,0:T(8,128)(2,1)S(1)}, u32[]{:S(2)}, u32[]{:S(2)}) collective-permute-start(bf16[128,1536]{1,0:T(8,128)(2,1)S(1)} %get-tuple-element.4), channel_id=1, source_target_pairs={{8,0},{16,8},{24,16},{9,1},{17,9},{25,17},{10,2},{18,10},{26,18},{... | collective-permute-start | bytes 1179656 | tf_op jit(solution)/shard_map/ppermute | solution.py:11
  484.0 213.4 %all-gather.45.cloned.1.call-start = ((), (), s32[]{:S(2)}) async-start(), calls=%async_computation.19 | async-start | bytes 1966080 | tf_op jit(solution)/shard_map/all_gather | solution.py:50
  484.6 277.7 %reduce-scatter.14.cloned.1.call-start = ((), (), s32[]{:S(2)}) async-start(), calls=%async_computation.13 | async-start | bytes 1966080 | tf_op jit(solution)/shard_map/reduce_scatter | solution.py:63
  506.7 19.4 %copy-start.3 = (bf16[128,6144]{1,0:T(8,128)(2,1)S(1)}, bf16[128,6144]{1,0:T(8,128)(2,1)}, u32[]{:S(2)}) copy-start(bf16[128,6144]{1,0:T(8,128)(2,1)} %all-gather.27.cloned.1.call-done) | copy-start | bytes 4718596
  506.7 19.4 %copy-start.7 = (bf16[1,1,128,1536]{3,2,1,0:T(8,128)(2,1)S(1)}, bf16[1,1,128,1536]{3,2,1,0:T(8,128)(2,1)}, u32[]{:S(2)}) copy-start(bf16[1,1,128,1536]{3,2,1,0:T(8,128)(2,1)} %copy-done.6) | copy-start | bytes 1179652
  526.1 20.5 %copy-start.16 = (bf16[128,1536]{1,0:T(8,128)(2,1)S(1)}, bf16[128,1536]{1,0:T(8,128)(2,1)}, u32[]{:S(2)}) copy-start(bf16[128,1536]{1,0:T(8,128)(2,1)} %reduce_sum.61) | copy-start | bytes 1179652
  541.1 22.3 %copy-start.4 = (bf16[128,6144]{1,0:T(8,128)(2,1)S(1)}, bf16[128,6144]{1,0:T(8,128)(2,1)}, u32[]{:S(2)}) copy-start(bf16[128,6144]{1,0:T(8,128)(2,1)} %all-gather.29.cloned.1.call-done) | copy-start | bytes 4718596
  541.1 22.3 %copy-start.9 = (bf16[1,1,128,1536]{3,2,1,0:T(8,128)(2,1)S(1)}, bf16[1,1,128,1536]{3,2,1,0:T(8,128)(2,1)}, u32[]{:S(2)}) copy-start(bf16[1,1,128,1536]{3,2,1,0:T(8,128)(2,1)} %copy-done.8) | copy-start | bytes 1179652
  563.4 21.3 %copy-start.17 = (bf16[128,1536]{1,0:T(8,128)(2,1)S(1)}, bf16[128,1536]{1,0:T(8,128)(2,1)}, u32[]{:S(2)}) copy-start(bf16[128,1536]{1,0:T(8,128)(2,1)} %reduce_sum.62) | copy-start | bytes 1179652
  578.6 22.8 %copy-start.5 = (bf16[128,6144]{1,0:T(8,128)(2,1)S(1)}, bf16[128,6144]{1,0:T(8,128)(2,1)}, u32[]{:S(2)}) copy-start(bf16[128,6144]{1,0:T(8,128)(2,1)} %all-gather.31.cloned.1.call-done) | copy-start | bytes 4718596
  578.6 22.8 %copy-start.10 = (bf16[1,1,128,1536]{3,2,1,0:T(8,128)(2,1)S(1)}, bf16[1,1,128,1536]{3,2,1,0:T(8,128)(2,1)}, u32[]{:S(2)}) copy-start(bf16[1,1,128,1536]{3,2,1,0:T(8,128)(2,1)} %all-gather.11) | copy-start | bytes 1179652
  601.4 20.7 %copy-start.18 = (bf16[128,1536]{1,0:T(8,128)(2,1)S(1)}, bf16[128,1536]{1,0:T(8,128)(2,1)}, u32[]{:S(2)}) copy-start(bf16[128,1536]{1,0:T(8,128)(2,1)} %reduce_sum.63) | copy-start | bytes 1179652
  639.0 43.8 %copy-start.14 = (bf16[1,1,128,1536]{3,2,1,0:T(8,128)(2,1)S(1)}, bf16[1,1,128,1536]{3,2,1,0:T(8,128)(2,1)}, u32[]{:S(2)}) copy-start(bf16[1,1,128,1536]{3,2,1,0:T(8,128)(2,1)} %all-gather.14) | copy-start | bytes 1179652
  693.5 36.9 %copy-start.1 = (bf16[128,6144]{1,0:T(8,128)(2,1)S(1)}, bf16[128,6144]{1,0:T(8,128)(2,1)}, u32[]{:S(2)}) copy-start(bf16[128,6144]{1,0:T(8,128)(2,1)} %all-gather.33.cloned.1.call-done) | copy-start | bytes 4718596
  730.4 31.8 %copy-start.13 = (bf16[128,1536]{1,0:T(8,128)(2,1)S(1)}, bf16[128,1536]{1,0:T(8,128)(2,1)}, u32[]{:S(2)}) copy-start(bf16[128,1536]{1,0:T(8,128)(2,1)} %bitcast_select_fusion.3) | copy-start | bytes 1179652
Sparse Core Ops, SparseCore 0:
  10.1 38.1 all-gather.34
  82.5 36.6 reduce-scatter.5
  131.1 33.5 all-gather.26
  200.6 36.6 reduce-scatter.7
  249.2 33.5 all-gather.28
  318.7 36.6 reduce-scatter.9
  367.0 33.5 all-gather.30
  435.6 36.6 reduce-scatter.11
  473.9 35.3 all-gather.36
  510.7 35.8 all-gather.38
  548.8 35.8 all-gather.40
  586.1 35.8 all-gather.42
  623.6 35.8 all-gather.32
  661.5 35.8 all-gather.44
  699.6 34.7 reduce-scatter.13
